TPU v7x, 32 devices: a whole 2x2x4 slice. The times are simulated.
32 devices in a mesh: batch: 4 (over y, x), ctx: 4 (over z), wt: 2 (over core).
Axes of the slice: x: 2, y: 2, z: 4, core: 2. Of those that a mesh axis runs over, the one named last changes fastest.
Arguments:
- inputs: bfloat16 [8, 512, 768], P(('batch', 'wt'), 'ctx'), may hold values from -6 to 6
- prefix_keys: bfloat16 [8, 20, 768], P(('batch', 'wt')), may hold values from -8 to 8
- prefix_values: bfloat16 [8, 20, 768], P(('batch', 'wt')), may hold values from -6 to 6
- gain_attn: bfloat16 [768], P('wt'), may hold values from 0.099609375 to 1.8984375
- w_query: bfloat16 [768, 768], P('wt'), may hold values from -0.02734375 to 0.02734375
- w_key: bfloat16 [768, 768], P('wt'), may hold values from -0.21875 to 0.21875
- w_value: bfloat16 [768, 768], P('wt'), may hold values from -0.21875 to 0.21875
- w_out: bfloat16 [768, 768], P('wt'), may hold values from -2.5 to 2.5
- bias_table: bfloat16 [32, 12], P('wt'), may hold values from -5 to 5
- gain_ffn: bfloat16 [768], P('wt'), may hold values from 0.099609375 to 1.8984375
- w_in: bfloat16 [768, 3072], P('wt'), may hold values from -0.21875 to 0.21875
- w_back: bfloat16 [3072, 768], P('wt'), may hold values from -0.15625 to 0.15625
- buckets: int32 [1023], replicated, may hold values from 0 to 31
- out_grad: bfloat16 [8, 512, 768], P(('batch', 'wt'), 'ctx'), may hold values from -6 to 6
Outputs:
- outputs: bfloat16 [8, 512, 768], P(('batch', 'wt'), 'ctx')
- grad_inputs: bfloat16 [8, 512, 768], P(('batch', 'wt'), 'ctx')
- grad_prefix_keys: float32 [8, 20, 768], P(('batch', 'wt'))
- grad_prefix_values: float32 [8, 20, 768], P(('batch', 'wt'))
- grad_gain_attn: float32 [768], P('wt')
- grad_gain_ffn: float32 [768], P('wt')
- grad_bias_table: float32 [32, 12], P('wt')
- grad_query: float32 [768, 768], P('wt')
- grad_key: float32 [768, 768], P('wt')
- grad_value: float32 [768, 768], P('wt')
- grad_out: float32 [768, 768], P('wt')
- grad_in: float32 [768, 3072], P('wt')
- grad_back: float32 [3072, 768], P('wt')
All inputs are finite; a program needn't handle non-finite values.
Results may differ from a plain program's by a relative error of at most 0.028.
Values may be sent and summed in bfloat16 or wider, within the bound.
No kernel may reach another device: no remote copies, remote signals or barrier semaphores. Data moves between devices by JAX's collectives and lax.ppermute only.
A program may use at most 128 MiB of HBM per device.

v0:
```python
import jax
import jax.numpy as jnp
from jax import lax
from jax.sharding import PartitionSpec as P

KB = 256
EPS = 1e-06


def times_t(left, right):
    return lax.dot_general(
        left, right, (((1,), (1,)), ((), ())), preferred_element_type=jnp.float32
    )


def t_times(left, right):
    return lax.dot_general(
        left, right, (((0,), (0,)), ((), ())), preferred_element_type=jnp.float32
    )


def norm_parts(values):
    inverse = lax.rsqrt(jnp.mean(values * values, axis=-1, keepdims=True) + EPS)
    return (values * inverse, inverse)


def norm_back(grad_norm, gain, scaled, inverse):
    grad_scaled = grad_norm * gain
    return inverse * (grad_scaled - scaled * jnp.mean(grad_scaled * scaled, axis=-1, keepdims=True))


def smooth_act(values):
    return jax.nn.gelu(values, approximate=True)


def shards(
    inputs,
    prefix_keys,
    prefix_values,
    gain_attn,
    w_query,
    w_key,
    w_value,
    w_out,
    bias_table,
    gain_ffn,
    w_in,
    w_back,
    buckets,
    out_grad,
):
    wq, wk, wv, wo, gain_one, table = (
        lax.all_gather(w_query, "wt", axis=0, tiled=True),
        lax.all_gather(w_key, "wt", axis=0, tiled=True),
        lax.all_gather(w_value, "wt", axis=0, tiled=True),
        lax.all_gather(w_out, "wt", axis=0, tiled=True),
        lax.all_gather(gain_attn, "wt", axis=0, tiled=True),
        lax.all_gather(bias_table, "wt", axis=0, tiled=True),
    )
    w_first, w_second, gain_two = (
        lax.all_gather(w_in, "wt", axis=0, tiled=True),
        lax.all_gather(w_back, "wt", axis=0, tiled=True),
        lax.all_gather(gain_ffn, "wt", axis=0, tiled=True),
    )
    tokens = inputs[0].astype(jnp.float32)
    rows, width = tokens.shape
    heads = table.shape[1]
    nbuck = table.shape[0]
    hsize = width // heads
    memory = prefix_keys.shape[1]
    keys_mem = prefix_keys[0].reshape(memory, heads, hsize)
    vals_mem = prefix_values[0].reshape(memory, heads, hsize)
    scaled1, inverse1 = norm_parts(tokens)
    normed1 = (scaled1 * gain_one.astype(jnp.float32)).astype(jnp.bfloat16)
    query = jnp.dot(normed1, wq, preferred_element_type=jnp.float32).astype(jnp.bfloat16)
    keys = jnp.dot(normed1, wk, preferred_element_type=jnp.float32).astype(jnp.bfloat16)
    vals = jnp.dot(normed1, wv, preferred_element_type=jnp.float32).astype(jnp.bfloat16)
    key_full, value_full = (
        lax.all_gather(keys, "ctx", axis=0, tiled=True),
        lax.all_gather(vals, "ctx", axis=0, tiled=True),
    )
    length = key_full.shape[0]
    starts = jnp.arange(length // KB, dtype=jnp.int32) * KB
    bucket_range = jnp.arange(nbuck, dtype=jnp.int32)
    positions = lax.axis_index("ctx") * rows + jnp.arange(rows, dtype=jnp.int32)
    qheads = query.reshape(rows, heads, hsize)

    def scores_at(start, key_all):
        key_block = lax.dynamic_slice_in_dim(key_all, start, KB, 0).reshape(KB, heads, hsize)
        cols = start + jnp.arange(KB, dtype=jnp.int32)
        where = cols[None, :] - positions[:, None] + (length - 1)
        bucket_ids = buckets[where]
        bucket_map = (bucket_ids[:, :, None] == bucket_range[None, None, :]).astype(jnp.bfloat16)
        bias = jnp.einsum("qkb,bh->hqk", bucket_map, table, preferred_element_type=jnp.float32)
        raw = jnp.einsum("qhd,khd->hqk", qheads, key_block, preferred_element_type=jnp.float32)
        return (raw + bias, bucket_map, key_block)

    mem_scores = jnp.einsum("qhd,khd->hqk", qheads, keys_mem, preferred_element_type=jnp.float32)
    top_start = jnp.max(mem_scores, axis=2)
    total_start = jnp.sum(jnp.exp(mem_scores - top_start[:, :, None]), axis=2)

    def stat_step(carry, start):
        top, total = carry
        block, _, _ = scores_at(start, key_full)
        new_top = jnp.maximum(top, jnp.max(block, axis=2))
        total = total * jnp.exp(top - new_top) + jnp.sum(
            jnp.exp(block - new_top[:, :, None]), axis=2
        )
        return ((new_top, total), None)

    (top, total), _ = lax.scan(stat_step, (top_start, total_start), starts)
    mem_prob = jnp.exp(mem_scores - top[:, :, None]) / total[:, :, None]
    mem_low = mem_prob.astype(jnp.bfloat16)
    mixed_start = jnp.einsum("hqk,khd->qhd", mem_low, vals_mem, preferred_element_type=jnp.float32)

    def out_step(acc, start):
        block, _, _ = scores_at(start, key_full)
        prob = (jnp.exp(block - top[:, :, None]) / total[:, :, None]).astype(jnp.bfloat16)
        value_block = lax.dynamic_slice_in_dim(value_full, start, KB, 0).reshape(KB, heads, hsize)
        return (
            acc + jnp.einsum("hqk,khd->qhd", prob, value_block, preferred_element_type=jnp.float32),
            None,
        )

    mixed, _ = lax.scan(out_step, mixed_start, starts)
    attended = mixed.reshape(rows, width).astype(jnp.bfloat16)
    hidden = tokens + jnp.dot(attended, wo, preferred_element_type=jnp.float32)
    scaled2, inverse2 = norm_parts(hidden)
    normed2 = (scaled2 * gain_two.astype(jnp.float32)).astype(jnp.bfloat16)
    inner = jnp.dot(normed2, w_first, preferred_element_type=jnp.float32)
    act_value, act_pull = jax.vjp(smooth_act, inner)
    act_out = act_value.astype(jnp.bfloat16)
    result = hidden + jnp.dot(act_out, w_second, preferred_element_type=jnp.float32)
    wq, wk, wv, wo, gain_one = (
        lax.all_gather(w_query, "wt", axis=0, tiled=True),
        lax.all_gather(w_key, "wt", axis=0, tiled=True),
        lax.all_gather(w_value, "wt", axis=0, tiled=True),
        lax.all_gather(w_out, "wt", axis=0, tiled=True),
        lax.all_gather(gain_attn, "wt", axis=0, tiled=True),
    )
    w_first, w_second, gain_two = (
        lax.all_gather(w_in, "wt", axis=0, tiled=True),
        lax.all_gather(w_back, "wt", axis=0, tiled=True),
        lax.all_gather(gain_ffn, "wt", axis=0, tiled=True),
    )
    key_back, value_back = (
        lax.all_gather(keys, "ctx", axis=0, tiled=True),
        lax.all_gather(vals, "ctx", axis=0, tiled=True),
    )
    cotangent = out_grad[0]
    grad_second = t_times(act_out, cotangent)
    grad_act = times_t(cotangent, w_second).astype(jnp.bfloat16)
    grad_inner = act_pull(grad_act.astype(jnp.float32))[0].astype(jnp.bfloat16)
    grad_first = t_times(normed2, grad_inner)
    grad_normed2 = times_t(grad_inner, w_first)
    grad_gain_two = jnp.sum(grad_normed2 * scaled2, axis=0)
    grad_hidden = cotangent.astype(jnp.float32) + norm_back(
        grad_normed2, gain_two.astype(jnp.float32), scaled2, inverse2
    )
    part_first, part_second, part_gain_two = (
        lax.psum_scatter(
            grad_first.astype(jnp.bfloat16), "wt", scatter_dimension=0, tiled=True
        ).astype(jnp.float32),
        lax.psum_scatter(
            grad_second.astype(jnp.bfloat16), "wt", scatter_dimension=0, tiled=True
        ).astype(jnp.float32),
        lax.psum_scatter(
            grad_gain_two.astype(jnp.bfloat16), "wt", scatter_dimension=0, tiled=True
        ).astype(jnp.float32),
    )
    grad_branch = grad_hidden.astype(jnp.bfloat16)
    grad_wo = t_times(attended, grad_branch)
    grad_mixed = times_t(grad_branch, wo).astype(jnp.bfloat16).reshape(rows, heads, hsize)
    spread = jnp.einsum("qhd,qhd->hq", grad_mixed.astype(jnp.float32), mixed)
    mem_dprob = jnp.einsum("qhd,khd->hqk", grad_mixed, vals_mem, preferred_element_type=jnp.float32)
    mem_dscore = (mem_prob * (mem_dprob - spread[:, :, None])).astype(jnp.bfloat16)
    grad_q_start = jnp.einsum(
        "hqk,khd->qhd", mem_dscore, keys_mem, preferred_element_type=jnp.float32
    )
    grad_mem_keys = jnp.einsum(
        "hqk,qhd->khd", mem_dscore, qheads, preferred_element_type=jnp.float32
    ).reshape(memory, width)
    grad_mem_values = jnp.einsum(
        "hqk,qhd->khd", mem_low, grad_mixed, preferred_element_type=jnp.float32
    ).reshape(memory, width)

    def grad_step(carry, start):
        grad_q, table_acc = carry
        block, bucket_map, key_block = scores_at(start, key_back)
        prob = jnp.exp(block - top[:, :, None]) / total[:, :, None]
        value_block = lax.dynamic_slice_in_dim(value_back, start, KB, 0).reshape(KB, heads, hsize)
        grad_prob = jnp.einsum(
            "qhd,khd->hqk", grad_mixed, value_block, preferred_element_type=jnp.float32
        )
        grad_score = (prob * (grad_prob - spread[:, :, None])).astype(jnp.bfloat16)
        grad_q = grad_q + jnp.einsum(
            "hqk,khd->qhd", grad_score, key_block, preferred_element_type=jnp.float32
        )
        grad_kblock = jnp.einsum(
            "hqk,qhd->khd", grad_score, qheads, preferred_element_type=jnp.float32
        ).reshape(KB, width)
        grad_vblock = jnp.einsum(
            "hqk,qhd->khd",
            prob.astype(jnp.bfloat16),
            grad_mixed,
            preferred_element_type=jnp.float32,
        ).reshape(KB, width)
        table_acc = table_acc + jnp.einsum(
            "hqk,qkb->bh", grad_score, bucket_map, preferred_element_type=jnp.float32
        )
        return ((grad_q, table_acc), (grad_kblock, grad_vblock))

    zero_table = jnp.zeros((nbuck, heads), jnp.float32)
    (grad_q, grad_table), (grad_kblocks, grad_vblocks) = lax.scan(
        grad_step, (grad_q_start, zero_table), starts
    )
    grad_key_all = grad_kblocks.reshape(length, width)
    grad_value_all = grad_vblocks.reshape(length, width)
    grad_key_own, grad_value_own = (
        lax.psum_scatter(
            grad_key_all.astype(jnp.bfloat16), "ctx", scatter_dimension=0, tiled=True
        ).astype(jnp.float32),
        lax.psum_scatter(
            grad_value_all.astype(jnp.bfloat16), "ctx", scatter_dimension=0, tiled=True
        ).astype(jnp.float32),
    )
    mem_key_total, mem_value_total = (
        lax.psum(grad_mem_keys.astype(jnp.bfloat16), "ctx").astype(jnp.float32),
        lax.psum(grad_mem_values.astype(jnp.bfloat16), "ctx").astype(jnp.float32),
    )
    grad_q_low = grad_q.reshape(rows, width).astype(jnp.bfloat16)
    grad_k_low = grad_key_own.astype(jnp.bfloat16)
    grad_v_low = grad_value_own.astype(jnp.bfloat16)
    grad_wq = t_times(normed1, grad_q_low)
    grad_wk = t_times(normed1, grad_k_low)
    grad_wv = t_times(normed1, grad_v_low)
    grad_normed1 = times_t(grad_q_low, wq) + times_t(grad_k_low, wk) + times_t(grad_v_low, wv)
    grad_gain_one = jnp.sum(grad_normed1 * scaled1, axis=0)
    grad_tokens = grad_hidden + norm_back(
        grad_normed1, gain_one.astype(jnp.float32), scaled1, inverse1
    )
    part_wq, part_wk, part_wv, part_wo, part_gain_one, part_table = (
        lax.psum_scatter(
            grad_wq.astype(jnp.bfloat16), "wt", scatter_dimension=0, tiled=True
        ).astype(jnp.float32),
        lax.psum_scatter(
            grad_wk.astype(jnp.bfloat16), "wt", scatter_dimension=0, tiled=True
        ).astype(jnp.float32),
        lax.psum_scatter(
            grad_wv.astype(jnp.bfloat16), "wt", scatter_dimension=0, tiled=True
        ).astype(jnp.float32),
        lax.psum_scatter(
            grad_wo.astype(jnp.bfloat16), "wt", scatter_dimension=0, tiled=True
        ).astype(jnp.float32),
        lax.psum_scatter(
            grad_gain_one.astype(jnp.bfloat16), "wt", scatter_dimension=0, tiled=True
        ).astype(jnp.float32),
        lax.psum_scatter(
            grad_table.astype(jnp.bfloat16), "wt", scatter_dimension=0, tiled=True
        ).astype(jnp.float32),
    )
    sums = (
        lax.psum(part_wq.astype(jnp.bfloat16), ("batch", "ctx")).astype(jnp.float32),
        lax.psum(part_wk.astype(jnp.bfloat16), ("batch", "ctx")).astype(jnp.float32),
        lax.psum(part_wv.astype(jnp.bfloat16), ("batch", "ctx")).astype(jnp.float32),
        lax.psum(part_wo.astype(jnp.bfloat16), ("batch", "ctx")).astype(jnp.float32),
        lax.psum(part_gain_one.astype(jnp.bfloat16), ("batch", "ctx")).astype(jnp.float32),
        lax.psum(part_table.astype(jnp.bfloat16), ("batch", "ctx")).astype(jnp.float32),
        lax.psum(part_first.astype(jnp.bfloat16), ("batch", "ctx")).astype(jnp.float32),
        lax.psum(part_second.astype(jnp.bfloat16), ("batch", "ctx")).astype(jnp.float32),
        lax.psum(part_gain_two.astype(jnp.bfloat16), ("batch", "ctx")).astype(jnp.float32),
    )
    return (
        result.astype(jnp.bfloat16)[None],
        grad_tokens.astype(jnp.bfloat16)[None],
        mem_key_total[None],
        mem_value_total[None],
        sums[4],
        sums[8],
        sums[5],
        sums[0],
        sums[1],
        sums[2],
        sums[3],
        sums[6],
        sums[7],
    )


def solution(mesh):
    in_specs = (
        P(("batch", "wt"), "ctx", None),
        P(("batch", "wt"), None, None),
        P(("batch", "wt"), None, None),
        P("wt"),
        P("wt", None),
        P("wt", None),
        P("wt", None),
        P("wt", None),
        P("wt", None),
        P("wt"),
        P("wt", None),
        P("wt", None),
        P(),
        P(("batch", "wt"), "ctx", None),
    )
    out_specs = (
        P(("batch", "wt"), "ctx", None),
        P(("batch", "wt"), "ctx", None),
        P(("batch", "wt"), None, None),
        P(("batch", "wt"), None, None),
        P("wt"),
        P("wt"),
        P("wt", None),
        P("wt", None),
        P("wt", None),
        P("wt", None),
        P("wt", None),
        P("wt", None),
        P("wt", None),
    )
    return jax.shard_map(shards, mesh=mesh, in_specs=in_specs, out_specs=out_specs, check_vma=False)
```

profile of v0, /device:TPU:0, one launch (start us, length us, event | category | flops | bytes accessed | tf_op | source)
XLA Modules:
  0.0 1362.5 jit_solution(13265489076617069256)
XLA Ops:
  24.0 9.5 all-gather.11.cloned.1.call-done
  35.2 19.8 %all_gather.46 = bf16[512,768]{1,0:T(8,128)(2,1)S(1)} all-gather(bf16[128,768]{1,0:T(8,128)(2,1)S(1)} %convolution_convert_fusion.9), channel_id=1, replica_groups=mesh['batch'=4,'ctx'=4,'wt'=2] {'ctx'}, dimensions={0}, use_global_device_ids=true | all-gather | bytes 983040 | tf_op jit(solution)/shard_map/all_gather | solution.py:79
  58.3 283.1 %while.47 = (s32[]{:T(128)}, f32[12,128]{1,0:T(8,128)}, f32[12,128]{1,0:T(8,128)}, s32[2]{0:T(128)S(1)}, bf16[512,768]{0,1:T(8,128)(2,1)S(1)}, /*index=5*/bf16[1...) while((s32[]{:T(128)}, f32[12,128]{1,0:T(8,128)}, ...), condition=%wide.region_6.7_spmd.clone, body=%wide.region_3.6_spmd.clone.sunk | while | flops 78318976 | bytes 12339127 | solution.py:111
  59.8 130.0 %gather_fusion = s32[32768]{0:T(1024)S(1)} fusion(s32[1023]{0:T(1024)S(1)} %get-tuple-element.1205, s32[32768]{0:T(1024)S(1)} %broadcast_clamp_fusion.6), kind=kCustom, calls=%fused_computation.clone.clone.1 | custom fusion | bytes 393216 | tf_op jit(solution)/shard_map/while/body/eval_jaxpr/gather | solution.py:92
  201.3 130.0 %gather_fusion = s32[32768]{0:T(1024)S(1)} fusion(s32[1023]{0:T(1024)S(1)} %get-tuple-element.1205, s32[32768]{0:T(1024)S(1)} %broadcast_clamp_fusion.6), kind=kCustom, calls=%fused_computation.clone.clone.1 | custom fusion | bytes 393216 | tf_op jit(solution)/shard_map/while/body/eval_jaxpr/gather | solution.py:92
  343.1 18.4 %all_gather.49 = bf16[512,768]{1,0:T(8,128)(2,1)S(1)} all-gather(bf16[128,768]{1,0:T(8,128)(2,1)S(1)} %convolution_convert_fusion.8), channel_id=1, replica_groups=mesh['batch'=4,'ctx'=4,'wt'=2] {'ctx'}, dimensions={0}, use_global_device_ids=true | all-gather | bytes 983040 | tf_op jit(solution)/shard_map/all_gather | solution.py:80
  364.4 284.0 %while.48 = (s32[]{:T(128)}, f32[128,12,64]{0,2,1:T(8,128)}, s32[2]{0:T(128)S(1)}, bf16[512,768]{0,1:T(8,128)(2,1)}, bf16[512,768]{0,1:T(8,128)(2,1)S(1)}, /*ind...) while((s32[]{:T(128)}, f32[128,12,64]{0,2,1:T(8,128)}, ...), condition=%wide.region_8.9_spmd.clone, body=%wide.region_7.8_spmd.clone.sunk | while | flops 128745856 | bytes 12664803 | solution.py:125
  370.1 130.0 %gather_fusion.1 = s32[32768]{0:T(1024)S(1)} fusion(s32[1023]{0:T(1024)S(1)} %get-tuple-element.1245, s32[32768]{0:T(1024)S(1)} %broadcast_clamp_fusion.7), kind=kCustom, calls=%fused_computation.1.clone.clone.1 | custom fusion | bytes 393216 | tf_op jit(solution)/shard_map/while/body/eval_jaxpr/gather | solution.py:92
  503.3 3.2 fusion.189
  512.1 130.0 %gather_fusion.1 = s32[32768]{0:T(1024)S(1)} fusion(s32[1023]{0:T(1024)S(1)} %get-tuple-element.1245, s32[32768]{0:T(1024)S(1)} %broadcast_clamp_fusion.7), kind=kCustom, calls=%fused_computation.1.clone.clone.1 | custom fusion | bytes 393216 | tf_op jit(solution)/shard_map/while/body/eval_jaxpr/gather | solution.py:92
  645.2 3.2 fusion.189
  651.4 3.3 fusion.92
  654.7 4.8 fusion.52
  668.4 294.8 %while.49 = (s32[]{:T(128)}, f32[128,12,64]{0,2,1:T(8,128)}, f32[32,12]{0,1:T(8,128)S(1)}, bf16[2,256,768]{2,1,0:T(8,128)(2,1)}, bf16[2,256,768]{2,1,0:T(8,128)(...) while((s32[]{:T(128)}, f32[128,12,64]{0,2,1:T(8,128)}, ...), condition=%wide.region_12.13_spmd.clone, body=%wide.region_11.12_spmd.clone.sunk | while | flops 307135616 | bytes 21652508 | solution.py:214
  672.0 130.0 %gather_fusion.2 = s32[32768]{0:T(1024)S(1)} fusion(s32[1023]{0:T(1024)S(1)} %get-tuple-element.1299, s32[32768]{0:T(1024)S(1)} %broadcast_clamp_fusion.8), kind=kCustom, calls=%fused_computation.2.clone.clone.1 | custom fusion | bytes 393216 | tf_op jit(solution)/shard_map/while/body/eval_jaxpr/gather | solution.py:92
  819.4 130.0 %gather_fusion.2 = s32[32768]{0:T(1024)S(1)} fusion(s32[1023]{0:T(1024)S(1)} %get-tuple-element.1299, s32[32768]{0:T(1024)S(1)} %broadcast_clamp_fusion.8), kind=kCustom, calls=%fused_computation.2.clone.clone.1 | custom fusion | bytes 393216 | tf_op jit(solution)/shard_map/while/body/eval_jaxpr/gather | solution.py:92
  968.4 17.5 %reduce-scatter.12.cloned.1.call-done = bf16[128,768]{1,0:T(8,128)(2,1)} async-done(((bf16[512,768]{1,0:T(8,128)(2,1)}), bf16[128,768]{1,0:T(8,128)(2,1)}) %reduce-scatter.12.cloned.1.call-update) | async-done | bytes 196624 | tf_op jit(solution)/shard_map/reduce_scatter | solution.py:220
  985.9 2.5 convolution_convert_fusion.5
  988.6 22.8 %reduce-scatter.14.cloned.1.call-done = bf16[128,768]{1,0:T(8,128)(2,1)} async-done(((bf16[512,768]{1,0:T(8,128)(2,1)}), bf16[128,768]{1,0:T(8,128)(2,1)}) %reduce-scatter.14.cloned.1.call-update) | async-done | bytes 196624 | tf_op jit(solution)/shard_map/reduce_scatter | solution.py:223
  1014.0 3.7 convolution_convert_fusion.1
  1019.1 3.8 convolution_convert_fusion
  1023.8 11.0 reduce-scatter.22.cloned.1.call-done
  1034.8 12.7 reduce-scatter.18.cloned.1.call-done
  1047.6 12.6 reduce-scatter.20.cloned.1.call-done
  1060.2 16.7 %reduce-scatter.24.cloned.1.call-done = bf16[384,3072]{1,0:T(8,128)(2,1)} async-done(((bf16[768,3072]{1,0:T(8,128)(2,1)}), bf16[384,3072]{1,0:T(8,128)(2,1)}) %reduce-scatter.24.cloned.1.call-update) | async-done | bytes 2359312 | tf_op jit(solution)/shard_map/reduce_scatter | solution.py:161
  1076.9 16.6 %reduce-scatter.26.cloned.1.call-done = bf16[1536,768]{1,0:T(8,128)(2,1)} async-done(((bf16[3072,768]{1,0:T(8,128)(2,1)}), bf16[1536,768]{1,0:T(8,128)(2,1)}) %reduce-scatter.26.cloned.1.call-update) | async-done | bytes 2359312 | tf_op jit(solution)/shard_map/reduce_scatter | solution.py:164
  1098.1 20.5 %all-reduce.4 = (bf16[1,20,768]{2,1,0:T(8,128)(2,1)S(1)}, bf16[1,20,768]{2,1,0:T(8,128)(2,1)S(1)}) all-reduce(bf16[1,20,768]{2,1,0:T(8,128)(2,1)S(1)} %broadcast_in_dim.44, bf16[1,20,768]{2,1,0:T(8,128)(2,1)S(1)} %broadcast_in_dim.55), channel_id=1, replica_groups=mesh['batch'=4,'ctx'=4,'wt'=2] {'ctx'}, use_global_device_ids=true, to_apply=%region_16.17 | all-reduce | flops 30720 | bytes 122880 | tf_op jit(solution)/shard_map/psum | solution.py:228
  1121.8 4.1 fusion.54
  1131.9 42.3 %all-reduce.2 = (bf16[16,12]{0,1:T(8,128)(2,1)S(1)}, bf16[384]{0:T(512)(128)(2,1)S(1)}, bf16[384]{0:T(512)(128)(2,1)S(1)}) all-reduce(bf16[16,12]{0,1:T(8,128)(2,1)S(1)} %copy.182, bf16[384]{0:T(512)(128)(2,1)S(1)} %dynamic-slice.1, bf16[384]{0:T(512)(128)(2,1)S(1)} %dynamic-slice.3), channel_id=1, replica_groups=mesh['batch'=4,'ctx'=4,'wt'=2] {'batch','ctx'}, use_global_device_ids=true, to_apply=%region_25.26 | all-reduce | flops 960 | bytes 3840 | tf_op jit(solution)/shard_map/psum | solution.py:268
  1176.9 168.2 %all-reduce.8.cloned.1.call-done = (bf16[384,768]{1,0:T(8,128)(2,1)}, bf16[384,768]{1,0:T(8,128)(2,1)}, bf16[384,768]{1,0:T(8,128)(2,1)}, bf16[384,768]{1,0:T(8,...) async-done(((bf16[384,768]{1,0:T(8,128)(2,1)}, bf16[384,768]{1,0:T(8,128)(2,1)}, bf16[384,768]{1,0:T(8,128)(2,1)}, bf16[384,768]{1,0:T(8,128)(2,1)}, ...) | async-done | bytes 7077904 | tf_op jit(solution)/shard_map/psum | solution.py:263
  1350.6 2.8 convert_element_type.265
  1353.4 2.5 convert_element_type.267
  (318 shorter events, 132.0 us)
Async XLA Ops:
  7.2 14.3 %all-gather.9.cloned.1.call-start = ((), (), s32[]{:S(2)}) async-start(), calls=%async_computation.9 | async-start | bytes 1769472 | tf_op jit(solution)/shard_map/all_gather | solution.py:53
  7.9 25.6 %all-gather.11.cloned.1.call-start = ((), (), s32[]{:S(2)}) async-start(), calls=%async_computation.10 | async-start | bytes 1769472 | tf_op jit(solution)/shard_map/all_gather | solution.py:54
  8.7 332.8 %all-gather.13.cloned.1.call-start = ((), (), s32[]{:S(2)}) async-start(), calls=%async_computation.11 | async-start | bytes 1769472 | tf_op jit(solution)/shard_map/all_gather | solution.py:55
  9.4 640.1 %all-gather.15.cloned.1.call-start = ((), (), s32[]{:S(2)}) async-start(), calls=%async_computation.12 | async-start | bytes 1769472 | tf_op jit(solution)/shard_map/all_gather | solution.py:56
  10.0 641.4 %all-gather.17.cloned.1.call-start = ((), (), s32[]{:S(2)}) async-start(), calls=%async_computation.13 | async-start | bytes 7077888 | tf_op jit(solution)/shard_map/all_gather | solution.py:61
  10.6 644.0 %all-gather.19.cloned.1.call-start = ((), (), s32[]{:S(2)}) async-start(), calls=%async_computation.14 | async-start | bytes 7077888 | tf_op jit(solution)/shard_map/all_gather | solution.py:62
  11.2 974.7 %reduce-scatter.12.cloned.1.call-start = ((), (), s32[]{:S(2)}) async-start(), calls=%async_computation.15 | async-start | bytes 983040 | tf_op jit(solution)/shard_map/reduce_scatter | solution.py:220
  14.0 21.1 %copy-start.36 = (f32[768]{0:T(1024)}, f32[768]{0:T(1024)S(1)}, u32[]{:S(2)}) copy-start(f32[768]{0:T(1024)S(1)} %reshape.355) | copy-start | bytes 9220
  14.2 21.0 %copy-start.47 = (f32[128]{0:T(128)}, f32[128]{0:T(128)S(1)}, u32[]{:S(2)}) copy-start(f32[128]{0:T(128)S(1)} %add_rsqrt_fusion.1) | copy-start | bytes 1540
  14.3 40.9 %copy-start.27 = (bf16[20,12,64]{2,1,0:T(8,128)(2,1)}, bf16[20,12,64]{2,1,0:T(8,128)(2,1)S(1)}, u32[]{:S(2)}) copy-start(bf16[20,12,64]{2,1,0:T(8,128)(2,1)S(1)} %reshape_squeeze.6) | copy-start | bytes 92164
  35.1 23.1 %copy-start = (s32[1023]{0:T(1024)S(1)}, s32[1023]{0:T(1024)}, u32[]{:S(2)}) copy-start(s32[1023]{0:T(1024)} %param.32) | copy-start | bytes 12280
  58.3 283.1 %copy-start.2 = (bf16[1,128,768]{2,1,0:T(8,128)(2,1)S(1)}, bf16[1,128,768]{2,1,0:T(8,128)(2,1)}, u32[]{:S(2)}) copy-start(bf16[1,128,768]{2,1,0:T(8,128)(2,1)} %param.20) | copy-start | bytes 589828
  58.3 283.1 %copy-start.37 = (f32[768]{0:T(1024)S(1)}, f32[768]{0:T(1024)}, u32[]{:S(2)}) copy-start(f32[768]{0:T(1024)} %copy-done.36) | copy-start | bytes 9220
  58.3 283.1 %copy-start.48 = (f32[128]{0:T(128)S(1)}, f32[128]{0:T(128)}, u32[]{:S(2)}) copy-start(f32[128]{0:T(128)} %copy-done.47) | copy-start | bytes 1540
  343.1 19.6 %copy-start.33 = (f32[12,128,20]{1,2,0:T(8,128)S(1)}, f32[12,128,20]{1,2,0:T(8,128)}, u32[]{:S(2)}) copy-start(f32[12,128,20]{1,2,0:T(8,128)} %copy-done.32) | copy-start | bytes 368644
  343.1 19.6 %copy-start.43 = (bf16[20,12,64]{2,1,0:T(8,128)(2,1)S(1)}, bf16[20,12,64]{2,1,0:T(8,128)(2,1)}, u32[]{:S(2)}) copy-start(bf16[20,12,64]{2,1,0:T(8,128)(2,1)} %reshape_squeeze.7) | copy-start | bytes 92164
  364.4 285.1 %copy-start.3 = (bf16[1,128,768]{2,1,0:T(8,128)(2,1)S(1)}, bf16[1,128,768]{2,1,0:T(8,128)(2,1)}, u32[]{:S(2)}) copy-start(bf16[1,128,768]{2,1,0:T(8,128)(2,1)} %param.20) | copy-start | bytes 589828
  651.3 10.6 copy-start.7
  651.3 10.6 copy-start.50
  963.3 48.2 %reduce-scatter.14.cloned.1.call-start = ((), (), s32[]{:S(2)}) async-start(), calls=%async_computation.16 | async-start | bytes 983040 | tf_op jit(solution)/shard_map/reduce_scatter | solution.py:223
  964.0 59.8 %reduce-scatter.16.cloned.1.call-start = ((), (), s32[]{:S(2)}) async-start(), calls=%async_computation.17 | async-start | bytes 1769472 | tf_op jit(solution)/shard_map/reduce_scatter | solution.py:243
  966.8 68.0 %reduce-scatter.22.cloned.1.call-start = ((), (), s32[]{:S(2)}) async-start(), calls=%async_computation.20 | async-start | bytes 1769472 | tf_op jit(solution)/shard_map/reduce_scatter | solution.py:252
  968.4 79.2 %reduce-scatter.18.cloned.1.call-start = ((), (), s32[]{:S(2)}) async-start(), calls=%async_computation.18 | async-start | bytes 1769472 | tf_op jit(solution)/shard_map/reduce_scatter | solution.py:246
  988.5 25.5 %copy-start.8 = (f32[128,768]{1,0:T(8,128)S(1)}, f32[128,768]{1,0:T(8,128)}, u32[]{:S(2)}) copy-start(f32[128,768]{1,0:T(8,128)} %copy-done.7) | copy-start | bytes 1179652
  988.5 25.5 %copy-start.17 = (bf16[128,3072]{1,0:T(8,128)(2,1)S(1)}, bf16[128,3072]{1,0:T(8,128)(2,1)}, u32[]{:S(2)}) copy-start(bf16[128,3072]{1,0:T(8,128)(2,1)} %copy-done.16) | copy-start | bytes 2359300
  988.5 25.5 %copy-start.42 = (f32[768]{0:T(1024)S(1)}, f32[768]{0:T(1024)}, u32[]{:S(2)}) copy-start(f32[768]{0:T(1024)} %reshape.356) | copy-start | bytes 9220
  988.5 25.5 %copy-start.51 = (f32[128]{0:T(128)S(1)}, f32[128]{0:T(128)}, u32[]{:S(2)}) copy-start(f32[128]{0:T(128)} %copy-done.50) | copy-start | bytes 1540
  988.5 71.7 %reduce-scatter.20.cloned.1.call-start = ((), (), s32[]{:S(2)}) async-start(), calls=%async_computation.19 | async-start | bytes 1769472 | tf_op jit(solution)/shard_map/reduce_scatter | solution.py:249
  1014.0 63.0 %reduce-scatter.24.cloned.1.call-start = ((), (), s32[]{:S(2)}) async-start(), calls=%async_computation.21 | async-start | bytes 7077888 | tf_op jit(solution)/shard_map/reduce_scatter | solution.py:161
  1017.7 75.8 %reduce-scatter.26.cloned.1.call-start = ((), (), s32[]{:S(2)}) async-start(), calls=%async_computation.22 | async-start | bytes 7077888 | tf_op jit(solution)/shard_map/reduce_scatter | solution.py:164
  1023.0 102.9 %reduce-scatter.28.cloned.1.call-start = ((), (), s32[]{:S(2)}) async-start(), calls=%async_computation.23 | async-start | bytes 12288
  1023.7 321.3 %all-reduce.8.cloned.1.call-start = ((), (), s32[]{:S(2)}) async-start(), calls=%async_computation.24 | async-start | bytes 14155776 | tf_op jit(solution)/shard_map/psum | solution.py:263
  (44 other events, 111.3 us)
Sparse Core Ops, SparseCore 0:
  9.6 11.9 all-gather.8
  23.1 10.3 all-gather.10
  35.0 10.3 all-gather.12
  46.9 10.3 all-gather.14
  58.7 15.5 all-gather.16
  75.7 15.6 all-gather.18
  963.4 22.5 reduce-scatter.11
  988.8 22.5 reduce-scatter.13
  1014.2 7.9 reduce-scatter.15
  1025.0 9.8 reduce-scatter.21
  1037.7 9.8 reduce-scatter.17
  1050.3 9.8 reduce-scatter.19
  1063.1 13.7 reduce-scatter.23
  1079.7 13.7 reduce-scatter.25
  1095.6 8.5 reduce-scatter.27
  1110.5 234.5 all-reduce.7
where the time goes:
time: 1360 us
  local copies, waits for them, and re-layouts  816 us (60%)
  waiting for transfers between devices  295 us (22%)
  blocking collectives  109 us (8%)
  matrix products  87.6 us (6%)
  other arithmetic  27.3 us (2%)
  between operations  15.4 us (1%)
    gather x14, local copies, waits for them, and re-layouts, scores_at(): bucket_ids = buckets[where]  781 us
    psum x1, waiting for transfers between devices, shards(): lax.psum(part_wq.astype(jnp.bfloat16), ('batch', 'ctx')).astype(jnp.float32)  168 us
    psum x1, blocking collectives, shards(): lax.psum(part_table.astype(jnp.bfloat16), ('batch', 'ctx'))  42.3 us
  transfers between devices with their start and end apart: 16, of which 10 were waited for; matrix products, arithmetic and copies ran while one was open for 45% of the time, Pallas kernels for 0%

commit v1 on v0

--- a/solution.py
+++ b/solution.py
@@ -260,7 +260,7 @@
         ).astype(jnp.float32),
     )
     sums = (
-        lax.psum(part_wq.astype(jnp.bfloat16), ("batch", "ctx")).astype(jnp.float32),
+        lax.psum(lax.psum(part_wq.astype(jnp.bfloat16), "ctx"), "batch").astype(jnp.float32),
         lax.psum(part_wk.astype(jnp.bfloat16), ("batch", "ctx")).astype(jnp.float32),
         lax.psum(part_wv.astype(jnp.bfloat16), ("batch", "ctx")).astype(jnp.float32),
         lax.psum(part_wo.astype(jnp.bfloat16), ("batch", "ctx")).astype(jnp.float32),

time: 1360 us -> 1450 us (1.066)
  waiting for transfers between devices: 295 us -> 375 us
    psum x1 -> x3, waiting for transfers between devices: 168 us -> 233 us  [the longest x1 205 us: shards(): lax.psum(part_wk.astype(jnp.bfloat16), ('batch', 'ctx')).astype(jnp.float32)]
  transfers between devices with their start and end apart: 16 -> 18, of which waited for: 10 -> 12; matrix products, arithmetic and copies ran while one was open for 45% -> 42% of each run, Pallas kernels for 0% -> 0%
where the time goes in v1:
time: 1450 us; the launch traced here: 1440 us
  local copies, waits for them, and re-layouts  817 us (56%)
  waiting for transfers between devices  375 us (26%)
  blocking collectives  106 us (7%)
  matrix products  89.7 us (6%)
  other arithmetic  28.4 us (2%)
  between operations  15.7 us (1%)
    gather x14, local copies, waits for them, and re-layouts, scores_at(): bucket_ids = buckets[where]  781 us
    psum x1, waiting for transfers between devices, shards(): lax.psum(part_wk.astype(jnp.bfloat16), ('batch', 'ctx')).astype(jnp.float32)  205 us
    psum x1, blocking collectives, shards(): lax.psum(part_table.astype(jnp.bfloat16), ('batch', 'ctx'))  39.3 us
  transfers between devices with their start and end apart: 18, of which 12 were waited for; matrix products, arithmetic and copies ran while one was open for 42% of the time, Pallas kernels for 0%

profile of v1, /device:TPU:0, one launch (start us, length us, event | category | flops | bytes accessed | tf_op | source)
XLA Modules:
  0.0 1444.6 jit_solution(11390016859340149961)
XLA Ops:
  24.0 9.5 all-gather.11.cloned.1.call-done
  35.2 19.8 %all_gather.46 = bf16[512,768]{1,0:T(8,128)(2,1)S(1)} all-gather(bf16[128,768]{1,0:T(8,128)(2,1)S(1)} %convolution_convert_fusion.9), channel_id=1, replica_groups=mesh['batch'=4,'ctx'=4,'wt'=2] {'ctx'}, dimensions={0}, use_global_device_ids=true | all-gather | bytes 983040 | tf_op jit(solution)/shard_map/all_gather | solution.py:79
  58.3 283.1 %while.47 = (s32[]{:T(128)}, f32[12,128]{1,0:T(8,128)}, f32[12,128]{1,0:T(8,128)}, s32[2]{0:T(128)S(1)}, bf16[512,768]{0,1:T(8,128)(2,1)S(1)}, /*index=5*/bf16[1...) while((s32[]{:T(128)}, f32[12,128]{1,0:T(8,128)}, ...), condition=%wide.region_6.7_spmd.clone, body=%wide.region_3.6_spmd.clone.sunk | while | flops 78318976 | bytes 12339127 | solution.py:111
  59.8 130.0 %gather_fusion = s32[32768]{0:T(1024)S(1)} fusion(s32[1023]{0:T(1024)S(1)} %get-tuple-element.1204, s32[32768]{0:T(1024)S(1)} %broadcast_clamp_fusion.6), kind=kCustom, calls=%fused_computation.clone.clone.1 | custom fusion | bytes 393216 | tf_op jit(solution)/shard_map/while/body/eval_jaxpr/gather | solution.py:92
  201.3 130.0 %gather_fusion = s32[32768]{0:T(1024)S(1)} fusion(s32[1023]{0:T(1024)S(1)} %get-tuple-element.1204, s32[32768]{0:T(1024)S(1)} %broadcast_clamp_fusion.6), kind=kCustom, calls=%fused_computation.clone.clone.1 | custom fusion | bytes 393216 | tf_op jit(solution)/shard_map/while/body/eval_jaxpr/gather | solution.py:92
  343.1 18.5 %all_gather.49 = bf16[512,768]{1,0:T(8,128)(2,1)S(1)} all-gather(bf16[128,768]{1,0:T(8,128)(2,1)S(1)} %convolution_convert_fusion.8), channel_id=1, replica_groups=mesh['batch'=4,'ctx'=4,'wt'=2] {'ctx'}, dimensions={0}, use_global_device_ids=true | all-gather | bytes 983040 | tf_op jit(solution)/shard_map/all_gather | solution.py:80
  364.4 284.0 %while.48 = (s32[]{:T(128)}, f32[128,12,64]{0,2,1:T(8,128)}, s32[2]{0:T(128)S(1)}, bf16[512,768]{0,1:T(8,128)(2,1)}, bf16[512,768]{0,1:T(8,128)(2,1)S(1)}, /*ind...) while((s32[]{:T(128)}, f32[128,12,64]{0,2,1:T(8,128)}, ...), condition=%wide.region_8.9_spmd.clone, body=%wide.region_7.8_spmd.clone.sunk | while | flops 128745856 | bytes 12664803 | solution.py:125
  370.1 130.0 %gather_fusion.1 = s32[32768]{0:T(1024)S(1)} fusion(s32[1023]{0:T(1024)S(1)} %get-tuple-element.1244, s32[32768]{0:T(1024)S(1)} %broadcast_clamp_fusion.7), kind=kCustom, calls=%fused_computation.1.clone.clone.1 | custom fusion | bytes 393216 | tf_op jit(solution)/shard_map/while/body/eval_jaxpr/gather | solution.py:92
  503.3 3.2 fusion.189
  512.1 130.0 %gather_fusion.1 = s32[32768]{0:T(1024)S(1)} fusion(s32[1023]{0:T(1024)S(1)} %get-tuple-element.1244, s32[32768]{0:T(1024)S(1)} %broadcast_clamp_fusion.7), kind=kCustom, calls=%fused_computation.1.clone.clone.1 | custom fusion | bytes 393216 | tf_op jit(solution)/shard_map/while/body/eval_jaxpr/gather | solution.py:92
  645.2 3.2 fusion.189
  651.4 3.3 fusion.92
  654.7 4.9 fusion.52
  668.4 296.4 %while.49 = (s32[]{:T(128)}, f32[128,12,64]{0,2,1:T(8,128)}, f32[32,12]{0,1:T(8,128)}, bf16[2,256,768]{2,1,0:T(8,128)(2,1)}, bf16[2,256,768]{2,1,0:T(8,128)(2,1)...) while((s32[]{:T(128)}, f32[128,12,64]{0,2,1:T(8,128)}, ...), condition=%wide.region_12.13_spmd.clone, body=%wide.region_11.12_spmd.clone.sunk | while | flops 307135616 | bytes 21652508 | solution.py:214
  672.2 130.0 %gather_fusion.2 = s32[32768]{0:T(1024)S(1)} fusion(s32[1023]{0:T(1024)S(1)} %get-tuple-element.1298, s32[32768]{0:T(1024)S(1)} %broadcast_clamp_fusion.8), kind=kCustom, calls=%fused_computation.2.clone.clone.1 | custom fusion | bytes 393216 | tf_op jit(solution)/shard_map/while/body/eval_jaxpr/gather | solution.py:92
  820.4 130.0 %gather_fusion.2 = s32[32768]{0:T(1024)S(1)} fusion(s32[1023]{0:T(1024)S(1)} %get-tuple-element.1298, s32[32768]{0:T(1024)S(1)} %broadcast_clamp_fusion.8), kind=kCustom, calls=%fused_computation.2.clone.clone.1 | custom fusion | bytes 393216 | tf_op jit(solution)/shard_map/while/body/eval_jaxpr/gather | solution.py:92
  970.0 6.7 reduce-scatter.16.cloned.1.call-done
  978.3 25.8 %reduce-scatter.12.cloned.1.call-done = bf16[128,768]{1,0:T(8,128)(2,1)} async-done(((bf16[512,768]{1,0:T(8,128)(2,1)}), bf16[128,768]{1,0:T(8,128)(2,1)}) %reduce-scatter.12.cloned.1.call-update) | async-done | bytes 196624 | tf_op jit(solution)/shard_map/reduce_scatter | solution.py:220
  1006.7 23.0 %reduce-scatter.14.cloned.1.call-done = bf16[128,768]{1,0:T(8,128)(2,1)} async-done(((bf16[512,768]{1,0:T(8,128)(2,1)}), bf16[128,768]{1,0:T(8,128)(2,1)}) %reduce-scatter.14.cloned.1.call-update) | async-done | bytes 196624 | tf_op jit(solution)/shard_map/reduce_scatter | solution.py:223
  1032.3 3.7 convolution_convert_fusion.1
  1037.5 3.8 convolution_convert_fusion
  1042.8 27.7 %all-reduce.10.cloned.1.call-done = bf16[384,768]{1,0:T(8,128)(2,1)} async-done(((bf16[384,768]{1,0:T(8,128)(2,1)}), bf16[384,768]{1,0:T(8,128)(2,1)}) %all-reduce.10.cloned.1.call-update) | async-done | bytes 589840 | tf_op jit(solution)/shard_map/psum | solution.py:263
  1070.5 11.2 reduce-scatter.22.cloned.1.call-done
  1081.7 12.5 reduce-scatter.18.cloned.1.call-done
  1094.3 12.8 reduce-scatter.20.cloned.1.call-done
  1107.1 16.6 %reduce-scatter.24.cloned.1.call-done = bf16[384,3072]{1,0:T(8,128)(2,1)} async-done(((bf16[768,3072]{1,0:T(8,128)(2,1)}), bf16[384,3072]{1,0:T(8,128)(2,1)}) %reduce-scatter.24.cloned.1.call-update) | async-done | bytes 2359312 | tf_op jit(solution)/shard_map/reduce_scatter | solution.py:161
  1123.7 16.6 %reduce-scatter.26.cloned.1.call-done = bf16[1536,768]{1,0:T(8,128)(2,1)} async-done(((bf16[3072,768]{1,0:T(8,128)(2,1)}), bf16[1536,768]{1,0:T(8,128)(2,1)}) %reduce-scatter.26.cloned.1.call-update) | async-done | bytes 2359312 | tf_op jit(solution)/shard_map/reduce_scatter | solution.py:164
  1144.8 20.5 %all-reduce.4 = (bf16[1,20,768]{2,1,0:T(8,128)(2,1)S(1)}, bf16[1,20,768]{2,1,0:T(8,128)(2,1)S(1)}) all-reduce(bf16[1,20,768]{2,1,0:T(8,128)(2,1)S(1)} %broadcast_in_dim.44, bf16[1,20,768]{2,1,0:T(8,128)(2,1)S(1)} %broadcast_in_dim.55), channel_id=1, replica_groups=mesh['batch'=4,'ctx'=4,'wt'=2] {'ctx'}, use_global_device_ids=true, to_apply=%region_16.17 | all-reduce | flops 30720 | bytes 122880 | tf_op jit(solution)/shard_map/psum | solution.py:228
  1168.5 4.1 fusion.54
  1178.6 39.3 %all-reduce.2 = (bf16[16,12]{0,1:T(8,128)(2,1)S(1)}, bf16[384]{0:T(512)(128)(2,1)S(1)}, bf16[384]{0:T(512)(128)(2,1)S(1)}) all-reduce(bf16[16,12]{0,1:T(8,128)(2,1)S(1)} %copy.182, bf16[384]{0:T(512)(128)(2,1)S(1)} %dynamic-slice.1, bf16[384]{0:T(512)(128)(2,1)S(1)} %dynamic-slice.3), channel_id=1, replica_groups=mesh['batch'=4,'ctx'=4,'wt'=2] {'batch','ctx'}, use_global_device_ids=true, to_apply=%region_25.26 | all-reduce | flops 960 | bytes 3840 | tf_op jit(solution)/shard_map/psum | solution.py:268
  1222.8 205.2 %all-reduce.14.cloned.1.call-done = (bf16[384,768]{1,0:T(8,128)(2,1)}, bf16[384,768]{1,0:T(8,128)(2,1)}, bf16[384,768]{1,0:T(8,128)(2,1)}, bf16[384,3072]{1,0:T(8,128)(2,1)}, bf16[1536,768]{1,0:T(8,128)(2,1)}) async-done(((bf16[384,768]{1,0:T(8,128)(2,1)}, bf16[384,768]{1,0:T(8,128)(2,1)}, bf16[384,768]{1,0:T(8,128)(2,1)}, bf16[384,3072]{1,0:T(8,128)(2,1)}, bf16[1536,768]{1,0:T(8,128)(2,1)}), ...) | async-done | bytes 6488080 | tf_op jit(solution)/shard_map/psum | solution.py:264
  1432.5 2.8 convert_element_type.265
  (322 shorter events, 141.8 us)
Async XLA Ops:
  7.2 14.3 all-gather.9.cloned.1.call-start
  7.9 25.6 %all-gather.11.cloned.1.call-start = ((), (), s32[]{:S(2)}) async-start(), calls=%async_computation.10 | async-start | bytes 1769472 | tf_op jit(solution)/shard_map/all_gather | solution.py:54
  8.7 332.7 %all-gather.13.cloned.1.call-start = ((), (), s32[]{:S(2)}) async-start(), calls=%async_computation.11 | async-start | bytes 1769472 | tf_op jit(solution)/shard_map/all_gather | solution.py:55
  9.4 640.1 %all-gather.15.cloned.1.call-start = ((), (), s32[]{:S(2)}) async-start(), calls=%async_computation.12 | async-start | bytes 1769472 | tf_op jit(solution)/shard_map/all_gather | solution.py:56
  10.0 641.4 %all-gather.17.cloned.1.call-start = ((), (), s32[]{:S(2)}) async-start(), calls=%async_computation.13 | async-start | bytes 7077888 | tf_op jit(solution)/shard_map/all_gather | solution.py:61
  10.6 644.1 %all-gather.19.cloned.1.call-start = ((), (), s32[]{:S(2)}) async-start(), calls=%async_computation.14 | async-start | bytes 7077888 | tf_op jit(solution)/shard_map/all_gather | solution.py:62
  11.2 965.4 %reduce-scatter.16.cloned.1.call-start = ((), (), s32[]{:S(2)}) async-start(), calls=%async_computation.17 | async-start | bytes 1769472 | tf_op jit(solution)/shard_map/reduce_scatter | solution.py:243
  14.0 21.1 %copy-start.35 = (f32[768]{0:T(1024)}, f32[768]{0:T(1024)S(1)}, u32[]{:S(2)}) copy-start(f32[768]{0:T(1024)S(1)} %reshape.355) | copy-start | bytes 9220
  14.3 40.9 %copy-start.27 = (bf16[20,12,64]{2,1,0:T(8,128)(2,1)}, bf16[20,12,64]{2,1,0:T(8,128)(2,1)S(1)}, u32[]{:S(2)}) copy-start(bf16[20,12,64]{2,1,0:T(8,128)(2,1)S(1)} %reshape_squeeze.6) | copy-start | bytes 92164
  35.1 23.1 %copy-start = (s32[1023]{0:T(1024)S(1)}, s32[1023]{0:T(1024)}, u32[]{:S(2)}) copy-start(s32[1023]{0:T(1024)} %param.32) | copy-start | bytes 12280
  58.3 283.1 %copy-start.2 = (bf16[1,128,768]{2,1,0:T(8,128)(2,1)S(1)}, bf16[1,128,768]{2,1,0:T(8,128)(2,1)}, u32[]{:S(2)}) copy-start(bf16[1,128,768]{2,1,0:T(8,128)(2,1)} %param.20) | copy-start | bytes 589828
  58.3 283.1 %copy-start.36 = (f32[768]{0:T(1024)S(1)}, f32[768]{0:T(1024)}, u32[]{:S(2)}) copy-start(f32[768]{0:T(1024)} %copy-done.35) | copy-start | bytes 9220
  58.3 283.1 %copy-start.47 = (f32[128]{0:T(128)S(1)}, f32[128]{0:T(128)}, u32[]{:S(2)}) copy-start(f32[128]{0:T(128)} %copy-done.46) | copy-start | bytes 1540
  364.4 285.1 %copy-start.3 = (bf16[1,128,768]{2,1,0:T(8,128)(2,1)S(1)}, bf16[1,128,768]{2,1,0:T(8,128)(2,1)}, u32[]{:S(2)}) copy-start(bf16[1,128,768]{2,1,0:T(8,128)(2,1)} %param.20) | copy-start | bytes 589828
  668.4 297.5 %copy-start.37 = (f32[768]{0:T(1024)S(1)}, f32[768]{0:T(1024)}, u32[]{:S(2)}) copy-start(f32[768]{0:T(1024)} %copy-done.35) | copy-start | bytes 9220
  668.4 297.5 %copy-start.48 = (f32[128]{0:T(128)S(1)}, f32[128]{0:T(128)}, u32[]{:S(2)}) copy-start(f32[128]{0:T(128)} %copy-done.46) | copy-start | bytes 1540
  968.4 35.7 %reduce-scatter.12.cloned.1.call-start = ((), (), s32[]{:S(2)}) async-start(), calls=%async_computation.15 | async-start | bytes 983040 | tf_op jit(solution)/shard_map/reduce_scatter | solution.py:220
  969.2 60.5 %reduce-scatter.14.cloned.1.call-start = ((), (), s32[]{:S(2)}) async-start(), calls=%async_computation.16 | async-start | bytes 983040 | tf_op jit(solution)/shard_map/reduce_scatter | solution.py:223
  969.9 100.5 %all-reduce.10.cloned.1.call-start = ((), (), s32[]{:S(2)}) async-start(), calls=%async_computation.18 | async-start | bytes 1179648 | tf_op jit(solution)/shard_map/psum | solution.py:263
  976.7 27.5 %copy-start.4 = (bf16[1,128,768]{2,1,0:T(8,128)(2,1)S(1)}, bf16[1,128,768]{2,1,0:T(8,128)(2,1)}, u32[]{:S(2)}) copy-start(bf16[1,128,768]{2,1,0:T(8,128)(2,1)} %param.20) | copy-start | bytes 589828
  976.7 105.1 %reduce-scatter.22.cloned.1.call-start = ((), (), s32[]{:S(2)}) async-start(), calls=%async_computation.22 | async-start | bytes 1769472 | tf_op jit(solution)/shard_map/reduce_scatter | solution.py:252
  978.2 116.0 %reduce-scatter.18.cloned.1.call-start = ((), (), s32[]{:S(2)}) async-start(), calls=%async_computation.20 | async-start | bytes 1769472 | tf_op jit(solution)/shard_map/reduce_scatter | solution.py:246
  1006.7 25.7 %copy-start.8 = (f32[128,768]{1,0:T(8,128)S(1)}, f32[128,768]{1,0:T(8,128)}, u32[]{:S(2)}) copy-start(f32[128,768]{1,0:T(8,128)} %copy-done.7) | copy-start | bytes 1179652
  1006.7 25.7 %copy-start.17 = (bf16[128,3072]{1,0:T(8,128)(2,1)S(1)}, bf16[128,3072]{1,0:T(8,128)(2,1)}, u32[]{:S(2)}) copy-start(bf16[128,3072]{1,0:T(8,128)(2,1)} %copy-done.16) | copy-start | bytes 2359300
  1006.7 25.7 %copy-start.41 = (f32[768]{0:T(1024)S(1)}, f32[768]{0:T(1024)}, u32[]{:S(2)}) copy-start(f32[768]{0:T(1024)} %reshape.356) | copy-start | bytes 9220
  1006.7 25.7 %copy-start.50 = (f32[128]{0:T(128)S(1)}, f32[128]{0:T(128)}, u32[]{:S(2)}) copy-start(f32[128]{0:T(128)} %copy-done.49) | copy-start | bytes 1540
  1006.7 100.4 %reduce-scatter.20.cloned.1.call-start = ((), (), s32[]{:S(2)}) async-start(), calls=%async_computation.21 | async-start | bytes 1769472 | tf_op jit(solution)/shard_map/reduce_scatter | solution.py:249
  1032.3 91.4 %reduce-scatter.24.cloned.1.call-start = ((), (), s32[]{:S(2)}) async-start(), calls=%async_computation.23 | async-start | bytes 7077888 | tf_op jit(solution)/shard_map/reduce_scatter | solution.py:161
  1036.1 104.2 %reduce-scatter.26.cloned.1.call-start = ((), (), s32[]{:S(2)}) async-start(), calls=%async_computation.24 | async-start | bytes 7077888 | tf_op jit(solution)/shard_map/reduce_scatter | solution.py:164
  1041.3 131.3 %reduce-scatter.28.cloned.1.call-start = ((), (), s32[]{:S(2)}) async-start(), calls=%async_computation.25 | async-start | bytes 12288
  1042.7 177.9 %all-reduce.12.cloned.1.call-start = ((), (), s32[]{:S(2)}) async-start(), calls=%async_computation.19 | async-start | bytes 1179648 | tf_op jit(solution)/shard_map/psum | solution.py:263
  1070.5 357.6 %all-reduce.14.cloned.1.call-start = ((), (), s32[]{:S(2)}) async-start(), calls=%async_computation.26 | async-start | bytes 12976128 | tf_op jit(solution)/shard_map/psum | solution.py:264
  (45 other events, 192.0 us)
Sparse Core Ops, SparseCore 0:
  9.6 11.9 all-gather.8
  23.1 10.3 all-gather.10
  35.0 10.3 all-gather.12
  46.9 10.3 all-gather.14
  58.7 15.5 all-gather.16
  75.7 15.6 all-gather.18
  968.6 8.0 reduce-scatter.15
  979.6 24.4 reduce-scatter.11
  1007.1 22.5 reduce-scatter.13
  1032.0 38.3 all-reduce.9
  1073.4 8.3 reduce-scatter.21
  1084.4 9.8 reduce-scatter.17
  1097.2 9.8 reduce-scatter.19
  1109.8 13.7 reduce-scatter.23
  1126.5 13.7 reduce-scatter.25
  1142.9 8.5 reduce-scatter.27
  1154.3 47.4 all-reduce.11
  1209.2 218.7 all-reduce.13
